TPU v7x, 256 devices: a whole 4x4x8 slice. The times are simulated.
256 devices in a mesh: row: 16 (over z_hi, x), col: 16 (over z_lo, y, core).
Axes of the slice: x: 4, y: 4, z: 8 (z_hi: 4, z_lo: 2; z = z_hi * 2 + z_lo), core: 2. Of those that a mesh axis runs over, the one named last changes fastest.
Arguments:
- features: bfloat16 [32768, 1024], P(('col', 'row')), may hold values from -6 to 6
- weight: bfloat16 [1024, 1024], P('col'), may hold values from -0.1875 to 0.1875
- tile_values: bfloat16 [16, 16, 16, 8, 128, 128], P('row', 'col'), may hold values from -0.0625 to 0.0625
- block_cols: int32 [16, 16, 16, 8], P('row', 'col'), may hold values from 0 to 15, as said below
- tile_counts: int32 [16, 16, 16], P('row', 'col'), may hold values from 1 to 8, as said below
Outputs:
- hidden_out: bfloat16 [32768, 1024], P(('row', 'col'))
Inputs may be any that keep to these rules, and one draw needn't show every extreme that they name: `block_cols`: the 8 entries of one block row of a tile are distinct block columns; values and block columns of slots that are not live are arbitrary. `tile_counts`: every tile has a block row with all 8 slots live.
All inputs are finite; a program needn't handle non-finite values.
Results may differ from a plain program's by a relative error of at most 0.019.
Values may be sent and summed in bfloat16 or wider, within the bound.
No kernel may reach another device: no remote copies, remote signals or barrier semaphores. Data moves between devices by JAX's collectives and lax.ppermute only.
A program may use at most 64 MiB of HBM per device.

v0:
```python
from functools import partial
import jax
import jax.numpy as jnp
from jax import lax
from jax.sharding import PartitionSpec as P


def aggregate(slot_values, slot_cols, slot_count, column_rows, group_size, offset, row_span):
    block_size = slot_values.shape[-1]
    slot_total = slot_values.shape[1]
    feat_width = column_rows.shape[-1]
    by_block = column_rows.reshape(-1, block_size, feat_width)
    row_count = row_span // block_size
    values_part = slot_values
    cols_part = slot_cols
    count_part = slot_count
    groups = row_count // group_size
    values_part = values_part.reshape(groups, group_size, slot_total, block_size, block_size)
    cols_part = cols_part.reshape(groups, group_size, slot_total)
    count_part = count_part.reshape(groups, group_size)

    def one_group(group_args):
        group_values, group_cols, group_count = group_args
        gathered = by_block[group_cols]
        live_slots = jnp.arange(slot_total, dtype=jnp.int32)[None, :] < group_count[:, None]
        masked = jnp.where(live_slots[:, :, None, None], group_values, jnp.zeros_like(group_values))
        return jnp.einsum("rsab,rsbf->raf", masked, gathered, preferred_element_type=jnp.float32)

    result = lax.map(one_group, (values_part, cols_part, count_part))
    return result.reshape(row_span, feat_width)


def body(features, weight, tile_values, block_cols, tile_counts):
    slot_values = tile_values[0, 0]
    slot_cols = block_cols[0, 0]
    slot_count = tile_counts[0, 0]
    out_rows = features.shape[0]
    block_size = slot_values.shape[-1]
    group_size = out_rows // block_size
    column_rows = lax.all_gather(features, "row", axis=0, tiled=True)
    partial_term = partial(aggregate, slot_values, slot_cols, slot_count, column_rows, group_size)
    summed = lax.psum_scatter(
        partial_term(jnp.int32(0), lax.axis_size("col") * out_rows).astype(jnp.bfloat16),
        "col",
        scatter_dimension=0,
        tiled=True,
    )
    product = jnp.dot(
        summed,
        lax.all_gather(weight, "col", axis=0, tiled=True),
        preferred_element_type=jnp.float32,
    )
    return jnp.maximum(product, 0.0).astype(jnp.bfloat16)


def solution(mesh):
    in_specs = (
        P(("col", "row"), None),
        P("col", None),
        P("row", "col", None, None, None, None),
        P("row", "col", None, None),
        P("row", "col", None),
    )
    out_specs = P(("row", "col"), None)
    return jax.shard_map(body, mesh=mesh, in_specs=in_specs, out_specs=out_specs, check_vma=False)
```

profile of v0, /device:TPU:2, one launch (start us, length us, event | category | flops | bytes accessed | tf_op | source)
XLA Modules:
  0.0 268.3 jit_solution(4133239872601638736)
XLA Ops:
  6.5 0.7 all-gather.3.cloned.1.call-update
  7.3 0.7 all-gather.5.cloned.1.call-update
  8.1 0.8 copy.6
  8.8 78.9 %all-gather.3.cloned.1.call-done = bf16[2048,1024]{1,0:T(8,128)(2,1)} async-done(((bf16[128,1024]{1,0:T(8,128)(2,1)}), bf16[2048,1024]{1,0:T(8,128)(2,1)}) %all-gather.3.cloned.1.call-update) | async-done | bytes 4194320 | tf_op jit(solution)/shard_map/all_gather | solution.py:40
  87.7 100.7 %while.10 = (s32[]{:T(128)}, bf16[16,1,128,1024]{3,2,1,0:T(8,128)(2,1)}, s32[16,1]{0,1:T(1,128)}, bf16[16,1,8,128,128]{4,3,2,1,0:T(8,128)(2,1)}, s32[16,1,8]{2,1...) while((s32[]{:T(128)}, bf16[16,1,128,1024]{3,2,1,0:T(8,128)(2,1)}, s32[16,1]{0,1:T(1,128)}, ...), condition=%wide.region_1.2_spmd, body=%wide.region_0.1_spmd.sunk | while | flops 268567584 | bytes 7083533 | solution.py:29
  87.7 2.9 %gather_fusion = bf16[8,128,1024]{2,1,0:T(8,128)(2,1)S(1)} fusion(bf16[16,128,1024]{2,1,0:T(8,128)(2,1)} %get-tuple-element.112, s32[1024]{0:T(1024)S(1)} %pad_clamp_fusion.2), kind=kCustom, calls=%fused_computation.clone.1 | custom fusion | bytes 4194336 | tf_op jit(solution)/shard_map/while/body/eval_jaxpr/gather | solution.py:24
  90.6 0.6 constant_dynamic-slice_fusion.3
  91.2 0.6 iota_compare_fusion.2
  91.8 2.2 fusion.17
  94.0 2.9 %gather_fusion = bf16[8,128,1024]{2,1,0:T(8,128)(2,1)S(1)} fusion(bf16[16,128,1024]{2,1,0:T(8,128)(2,1)} %get-tuple-element.112, s32[1024]{0:T(1024)S(1)} %pad_clamp_fusion.2), kind=kCustom, calls=%fused_computation.clone.1 | custom fusion | bytes 4194336 | tf_op jit(solution)/shard_map/while/body/eval_jaxpr/gather | solution.py:24
  96.9 0.6 constant_dynamic-slice_fusion.3
  97.5 0.6 iota_compare_fusion.2
  98.1 2.2 fusion.17
  100.3 3.0 %gather_fusion = bf16[8,128,1024]{2,1,0:T(8,128)(2,1)S(1)} fusion(bf16[16,128,1024]{2,1,0:T(8,128)(2,1)} %get-tuple-element.112, s32[1024]{0:T(1024)S(1)} %pad_clamp_fusion.2), kind=kCustom, calls=%fused_computation.clone.1 | custom fusion | bytes 4194336 | tf_op jit(solution)/shard_map/while/body/eval_jaxpr/gather | solution.py:24
  103.3 0.6 constant_dynamic-slice_fusion.3
  103.9 0.6 iota_compare_fusion.2
  104.5 2.2 fusion.17
  106.7 2.9 %gather_fusion = bf16[8,128,1024]{2,1,0:T(8,128)(2,1)S(1)} fusion(bf16[16,128,1024]{2,1,0:T(8,128)(2,1)} %get-tuple-element.112, s32[1024]{0:T(1024)S(1)} %pad_clamp_fusion.2), kind=kCustom, calls=%fused_computation.clone.1 | custom fusion | bytes 4194336 | tf_op jit(solution)/shard_map/while/body/eval_jaxpr/gather | solution.py:24
  109.6 0.6 constant_dynamic-slice_fusion.3
  110.2 0.6 iota_compare_fusion.2
  110.8 2.2 fusion.17
  113.0 2.9 %gather_fusion = bf16[8,128,1024]{2,1,0:T(8,128)(2,1)S(1)} fusion(bf16[16,128,1024]{2,1,0:T(8,128)(2,1)} %get-tuple-element.112, s32[1024]{0:T(1024)S(1)} %pad_clamp_fusion.2), kind=kCustom, calls=%fused_computation.clone.1 | custom fusion | bytes 4194336 | tf_op jit(solution)/shard_map/while/body/eval_jaxpr/gather | solution.py:24
  115.9 0.6 constant_dynamic-slice_fusion.3
  116.5 0.6 iota_compare_fusion.2
  117.1 2.2 fusion.17
  119.3 2.9 %gather_fusion = bf16[8,128,1024]{2,1,0:T(8,128)(2,1)S(1)} fusion(bf16[16,128,1024]{2,1,0:T(8,128)(2,1)} %get-tuple-element.112, s32[1024]{0:T(1024)S(1)} %pad_clamp_fusion.2), kind=kCustom, calls=%fused_computation.clone.1 | custom fusion | bytes 4194336 | tf_op jit(solution)/shard_map/while/body/eval_jaxpr/gather | solution.py:24
  122.2 0.6 constant_dynamic-slice_fusion.3
  122.8 0.6 iota_compare_fusion.2
  123.4 2.2 fusion.17
  125.6 2.9 %gather_fusion = bf16[8,128,1024]{2,1,0:T(8,128)(2,1)S(1)} fusion(bf16[16,128,1024]{2,1,0:T(8,128)(2,1)} %get-tuple-element.112, s32[1024]{0:T(1024)S(1)} %pad_clamp_fusion.2), kind=kCustom, calls=%fused_computation.clone.1 | custom fusion | bytes 4194336 | tf_op jit(solution)/shard_map/while/body/eval_jaxpr/gather | solution.py:24
  129.1 0.6 iota_compare_fusion.2
  129.7 2.1 fusion.17
  131.8 2.9 %gather_fusion = bf16[8,128,1024]{2,1,0:T(8,128)(2,1)S(1)} fusion(bf16[16,128,1024]{2,1,0:T(8,128)(2,1)} %get-tuple-element.112, s32[1024]{0:T(1024)S(1)} %pad_clamp_fusion.2), kind=kCustom, calls=%fused_computation.clone.1 | custom fusion | bytes 4194336 | tf_op jit(solution)/shard_map/while/body/eval_jaxpr/gather | solution.py:24
  135.3 0.6 iota_compare_fusion.2
  136.0 2.1 fusion.17
  138.1 2.9 %gather_fusion = bf16[8,128,1024]{2,1,0:T(8,128)(2,1)S(1)} fusion(bf16[16,128,1024]{2,1,0:T(8,128)(2,1)} %get-tuple-element.112, s32[1024]{0:T(1024)S(1)} %pad_clamp_fusion.2), kind=kCustom, calls=%fused_computation.clone.1 | custom fusion | bytes 4194336 | tf_op jit(solution)/shard_map/while/body/eval_jaxpr/gather | solution.py:24
  141.6 0.6 iota_compare_fusion.2
  142.2 2.1 fusion.17
  144.4 2.9 %gather_fusion = bf16[8,128,1024]{2,1,0:T(8,128)(2,1)S(1)} fusion(bf16[16,128,1024]{2,1,0:T(8,128)(2,1)} %get-tuple-element.112, s32[1024]{0:T(1024)S(1)} %pad_clamp_fusion.2), kind=kCustom, calls=%fused_computation.clone.1 | custom fusion | bytes 4194336 | tf_op jit(solution)/shard_map/while/body/eval_jaxpr/gather | solution.py:24
  147.9 0.6 iota_compare_fusion.2
  148.5 2.2 fusion.17
  150.7 2.9 %gather_fusion = bf16[8,128,1024]{2,1,0:T(8,128)(2,1)S(1)} fusion(bf16[16,128,1024]{2,1,0:T(8,128)(2,1)} %get-tuple-element.112, s32[1024]{0:T(1024)S(1)} %pad_clamp_fusion.2), kind=kCustom, calls=%fused_computation.clone.1 | custom fusion | bytes 4194336 | tf_op jit(solution)/shard_map/while/body/eval_jaxpr/gather | solution.py:24
  154.1 0.6 iota_compare_fusion.2
  154.8 2.2 fusion.17
  156.9 2.9 %gather_fusion = bf16[8,128,1024]{2,1,0:T(8,128)(2,1)S(1)} fusion(bf16[16,128,1024]{2,1,0:T(8,128)(2,1)} %get-tuple-element.112, s32[1024]{0:T(1024)S(1)} %pad_clamp_fusion.2), kind=kCustom, calls=%fused_computation.clone.1 | custom fusion | bytes 4194336 | tf_op jit(solution)/shard_map/while/body/eval_jaxpr/gather | solution.py:24
  159.8 0.6 constant_dynamic-slice_fusion.3
  160.4 0.6 iota_compare_fusion.2
  161.1 2.2 fusion.17
  163.2 2.9 %gather_fusion = bf16[8,128,1024]{2,1,0:T(8,128)(2,1)S(1)} fusion(bf16[16,128,1024]{2,1,0:T(8,128)(2,1)} %get-tuple-element.112, s32[1024]{0:T(1024)S(1)} %pad_clamp_fusion.2), kind=kCustom, calls=%fused_computation.clone.1 | custom fusion | bytes 4194336 | tf_op jit(solution)/shard_map/while/body/eval_jaxpr/gather | solution.py:24
  166.1 0.6 constant_dynamic-slice_fusion.3
  166.7 0.6 iota_compare_fusion.2
  167.4 2.2 fusion.17
  169.5 2.9 %gather_fusion = bf16[8,128,1024]{2,1,0:T(8,128)(2,1)S(1)} fusion(bf16[16,128,1024]{2,1,0:T(8,128)(2,1)} %get-tuple-element.112, s32[1024]{0:T(1024)S(1)} %pad_clamp_fusion.2), kind=kCustom, calls=%fused_computation.clone.1 | custom fusion | bytes 4194336 | tf_op jit(solution)/shard_map/while/body/eval_jaxpr/gather | solution.py:24
  172.4 0.6 constant_dynamic-slice_fusion.3
  173.0 0.6 iota_compare_fusion.2
  173.6 2.1 fusion.17
  175.8 2.9 %gather_fusion = bf16[8,128,1024]{2,1,0:T(8,128)(2,1)S(1)} fusion(bf16[16,128,1024]{2,1,0:T(8,128)(2,1)} %get-tuple-element.112, s32[1024]{0:T(1024)S(1)} %pad_clamp_fusion.2), kind=kCustom, calls=%fused_computation.clone.1 | custom fusion | bytes 4194336 | tf_op jit(solution)/shard_map/while/body/eval_jaxpr/gather | solution.py:24
  179.3 0.6 iota_compare_fusion.2
  179.9 2.1 fusion.17
  182.1 2.9 %gather_fusion = bf16[8,128,1024]{2,1,0:T(8,128)(2,1)S(1)} fusion(bf16[16,128,1024]{2,1,0:T(8,128)(2,1)} %get-tuple-element.112, s32[1024]{0:T(1024)S(1)} %pad_clamp_fusion.2), kind=kCustom, calls=%fused_computation.clone.1 | custom fusion | bytes 4194336 | tf_op jit(solution)/shard_map/while/body/eval_jaxpr/gather | solution.py:24
  185.5 0.6 iota_compare_fusion.2
  186.2 2.2 fusion.17
  188.4 70.5 %reduce-scatter.2.cloned.1.call-done = bf16[128,1024]{1,0:T(8,128)(2,1)} async-done(((bf16[2048,1024]{1,0:T(8,128)(2,1)}), bf16[128,1024]{1,0:T(8,128)(2,1)}) %reduce-scatter.2.cloned.1.call-update) | async-done | bytes 262160 | tf_op jit(solution)/shard_map/reduce_scatter | solution.py:42
  258.9 2.8 %fusion.8 = bf16[128,1024]{1,0:T(8,128)(2,1)} fusion(bf16[128,1024]{1,0:T(8,128)(2,1)} %reduce-scatter.2.cloned.1.call-done, bf16[1024,1024]{1,0:T(8,128)(2,1)} %all-gather.5.cloned.1.call-done), kind=kOutput, calls=%fused_computation.17 | convolution fusion | flops 268697600 | bytes 2621440 | tf_op jit(solution)/shard_map/dot_general | solution.py:48
  (77 shorter events, 4.5 us)
Async XLA Ops:
  6.5 81.2 %all-gather.3.cloned.1.call-start = ((), (), s32[]{:S(2)}) async-start(), calls=%async_computation.1 | async-start | bytes 4456448 | tf_op jit(solution)/shard_map/all_gather | solution.py:40
  7.3 181.2 %all-gather.5.cloned.1.call-start = ((), (), s32[]{:S(2)}) async-start(), calls=%async_computation.3 | async-start | bytes 2228224 | tf_op jit(solution)/shard_map/all_gather | solution.py:50
  8.0 250.9 %reduce-scatter.2.cloned.1.call-start = ((), (), s32[]{:S(2)}) async-start(), calls=%async_computation.2 | async-start | bytes 4456448 | tf_op jit(solution)/shard_map/reduce_scatter | solution.py:42
  87.7 2.9 %copy-start = (s32[16,1]{0,1:T(1,128)S(1)}, s32[16,1]{0,1:T(1,128)}, u32[]{:S(2)}) copy-start(s32[16,1]{0,1:T(1,128)} %get-tuple-element.109) | copy-start | bytes 196 | tf_op jit(solution)/shard_map/while
  94.0 2.9 %copy-start = (s32[16,1]{0,1:T(1,128)S(1)}, s32[16,1]{0,1:T(1,128)}, u32[]{:S(2)}) copy-start(s32[16,1]{0,1:T(1,128)} %get-tuple-element.109) | copy-start | bytes 196 | tf_op jit(solution)/shard_map/while
  100.3 3.0 %copy-start = (s32[16,1]{0,1:T(1,128)S(1)}, s32[16,1]{0,1:T(1,128)}, u32[]{:S(2)}) copy-start(s32[16,1]{0,1:T(1,128)} %get-tuple-element.109) | copy-start | bytes 196 | tf_op jit(solution)/shard_map/while
  106.7 2.9 %copy-start = (s32[16,1]{0,1:T(1,128)S(1)}, s32[16,1]{0,1:T(1,128)}, u32[]{:S(2)}) copy-start(s32[16,1]{0,1:T(1,128)} %get-tuple-element.109) | copy-start | bytes 196 | tf_op jit(solution)/shard_map/while
  113.0 2.9 %copy-start = (s32[16,1]{0,1:T(1,128)S(1)}, s32[16,1]{0,1:T(1,128)}, u32[]{:S(2)}) copy-start(s32[16,1]{0,1:T(1,128)} %get-tuple-element.109) | copy-start | bytes 196 | tf_op jit(solution)/shard_map/while
  119.3 2.9 %copy-start = (s32[16,1]{0,1:T(1,128)S(1)}, s32[16,1]{0,1:T(1,128)}, u32[]{:S(2)}) copy-start(s32[16,1]{0,1:T(1,128)} %get-tuple-element.109) | copy-start | bytes 196 | tf_op jit(solution)/shard_map/while
  125.6 2.9 %copy-start = (s32[16,1]{0,1:T(1,128)S(1)}, s32[16,1]{0,1:T(1,128)}, u32[]{:S(2)}) copy-start(s32[16,1]{0,1:T(1,128)} %get-tuple-element.109) | copy-start | bytes 196 | tf_op jit(solution)/shard_map/while
  131.8 2.9 %copy-start = (s32[16,1]{0,1:T(1,128)S(1)}, s32[16,1]{0,1:T(1,128)}, u32[]{:S(2)}) copy-start(s32[16,1]{0,1:T(1,128)} %get-tuple-element.109) | copy-start | bytes 196 | tf_op jit(solution)/shard_map/while
  138.1 2.9 %copy-start = (s32[16,1]{0,1:T(1,128)S(1)}, s32[16,1]{0,1:T(1,128)}, u32[]{:S(2)}) copy-start(s32[16,1]{0,1:T(1,128)} %get-tuple-element.109) | copy-start | bytes 196 | tf_op jit(solution)/shard_map/while
  144.4 2.9 %copy-start = (s32[16,1]{0,1:T(1,128)S(1)}, s32[16,1]{0,1:T(1,128)}, u32[]{:S(2)}) copy-start(s32[16,1]{0,1:T(1,128)} %get-tuple-element.109) | copy-start | bytes 196 | tf_op jit(solution)/shard_map/while
  150.6 2.9 %copy-start = (s32[16,1]{0,1:T(1,128)S(1)}, s32[16,1]{0,1:T(1,128)}, u32[]{:S(2)}) copy-start(s32[16,1]{0,1:T(1,128)} %get-tuple-element.109) | copy-start | bytes 196 | tf_op jit(solution)/shard_map/while
  156.9 2.9 %copy-start = (s32[16,1]{0,1:T(1,128)S(1)}, s32[16,1]{0,1:T(1,128)}, u32[]{:S(2)}) copy-start(s32[16,1]{0,1:T(1,128)} %get-tuple-element.109) | copy-start | bytes 196 | tf_op jit(solution)/shard_map/while
  163.2 2.9 %copy-start = (s32[16,1]{0,1:T(1,128)S(1)}, s32[16,1]{0,1:T(1,128)}, u32[]{:S(2)}) copy-start(s32[16,1]{0,1:T(1,128)} %get-tuple-element.109) | copy-start | bytes 196 | tf_op jit(solution)/shard_map/while
  169.5 2.9 %copy-start = (s32[16,1]{0,1:T(1,128)S(1)}, s32[16,1]{0,1:T(1,128)}, u32[]{:S(2)}) copy-start(s32[16,1]{0,1:T(1,128)} %get-tuple-element.109) | copy-start | bytes 196 | tf_op jit(solution)/shard_map/while
  175.8 2.9 %copy-start = (s32[16,1]{0,1:T(1,128)S(1)}, s32[16,1]{0,1:T(1,128)}, u32[]{:S(2)}) copy-start(s32[16,1]{0,1:T(1,128)} %get-tuple-element.109) | copy-start | bytes 196 | tf_op jit(solution)/shard_map/while
  182.0 2.9 %copy-start = (s32[16,1]{0,1:T(1,128)S(1)}, s32[16,1]{0,1:T(1,128)}, u32[]{:S(2)}) copy-start(s32[16,1]{0,1:T(1,128)} %get-tuple-element.109) | copy-start | bytes 196 | tf_op jit(solution)/shard_map/while
Sparse Core Ops, SparseCore 0:
  9.8 77.9 all-gather.2
  89.6 36.9 all-gather.4
  188.5 70.3 reduce-scatter.1
where the time goes:
time: 269 us; the launch traced here: 268 us
  waiting for transfers between devices  151 us (56%)
  local copies, waits for them, and re-layouts  56.3 us (21%)
  matrix products  37.4 us (14%)
  between operations  13.1 us (5%)
  other arithmetic  10.1 us (4%)
    all_gather x1, waiting for transfers between devices, body(): column_rows = lax.all_gather(features, 'row', axis=0, tiled=True)  78.9 us
    reduce_scatter x1, waiting for transfers between devices, body(): lax.psum_scatter(partial_term(jnp.int32(0), lax.axis_size('col') * out_ro...  70.5 us
    gather x16, local copies, waits for them, and re-layouts, one_group(): gathered = by_block[group_cols]  46 us
    dot_general x16, matrix products, one_group(): jnp.einsum('rsab,rsbf->raf', masked, gathered, preferred_element_type=jnp...  34.6 us
    lt x16, other arithmetic, one_group(): jnp.arange(slot_total, dtype=jnp.int32)[None, :] < group_count[:, None]  9.91 us
    dynamic_slice x16, local copies, waits for them, and re-layouts, aggregate(): result = lax.map(one_group, (values_part, cols_part, count_part))  9.52 us
  transfers between devices with their start and end apart: 3, of which 2 were waited for; matrix products, arithmetic and copies ran while one was open for 38% of the time, Pallas kernels for 0%

commit v1 on v0

--- a/solution.py
+++ b/solution.py
@@ -37,7 +37,12 @@
     out_rows = features.shape[0]
     block_size = slot_values.shape[-1]
     group_size = out_rows // block_size
-    column_rows = lax.all_gather(features, "row", axis=0, tiled=True)
+    column_rows = jnp.concatenate(
+        lax.all_to_all(
+            jnp.stack(lax.axis_size("row") * [features]), "row", split_axis=0, concat_axis=0
+        ),
+        axis=0,
+    )
     partial_term = partial(aggregate, slot_values, slot_cols, slot_count, column_rows, group_size)
     summed = lax.psum_scatter(
         partial_term(jnp.int32(0), lax.axis_size("col") * out_rows).astype(jnp.bfloat16),

time: 269 us -> 306 us (1.14)
  waiting for transfers between devices: 151 us -> 172 us
  starting transfers between devices: 0.08 us -> 11.7 us
    all_to_all x0 -> x1, waiting for transfers between devices: none -> 104 us  [body(): lax.all_to_all(jnp.stack(lax.axis_size('row') * [features]), 'row', split...]
    all_gather x1 -> x0, waiting for transfers between devices: 78.9 us -> none  [body(): column_rows = lax.all_gather(features, 'row', axis=0, tiled=True)]
    all_to_all x0 -> x1, starting transfers between devices: none -> 11.6 us  [body(): lax.all_to_all(jnp.stack(lax.axis_size('row') * [features]), 'row', split...]
    another operation x0 -> x1, local copies, waits for them, and re-layouts: none -> 3.46 us  [body(): jnp.stack(lax.axis_size('row') * [features])]
    reduce_scatter x1, waiting for transfers between devices: 70.5 us -> 67 us  [body(): lax.psum_scatter(partial_term(jnp.int32(0), lax.axis_size('col') * out_ro...]
  transfers between devices with their start and end apart: 3 -> 3, of which waited for: 2 -> 2; matrix products, arithmetic and copies ran while one was open for 38% -> 33% of each run, Pallas kernels for 0% -> 0%
where the time goes in v1:
time: 306 us; the launch traced here: 304 us
  waiting for transfers between devices  172 us (56%)
  local copies, waits for them, and re-layouts  59 us (19%)
  matrix products  37.4 us (12%)
  between operations  13.4 us (4%)
  starting transfers between devices  11.7 us (4%)
  other arithmetic  10.1 us (3%)
    all_to_all x1, waiting for transfers between devices, body(): lax.all_to_all(jnp.stack(lax.axis_size('row') * [features]), 'row', split...  104 us
    reduce_scatter x1, waiting for transfers between devices, body(): lax.psum_scatter(partial_term(jnp.int32(0), lax.axis_size('col') * out_ro...  67 us
    gather x16, local copies, waits for them, and re-layouts, one_group(): gathered = by_block[group_cols]  45.9 us
    dot_general x16, matrix products, one_group(): jnp.einsum('rsab,rsbf->raf', masked, gathered, preferred_element_type=jnp...  34.6 us
    all_to_all x1, starting transfers between devices, body(): lax.all_to_all(jnp.stack(lax.axis_size('row') * [features]), 'row', split...  11.6 us
    lt x16, other arithmetic, one_group(): jnp.arange(slot_total, dtype=jnp.int32)[None, :] < group_count[:, None]  9.96 us
    dynamic_slice x16, local copies, waits for them, and re-layouts, aggregate(): result = lax.map(one_group, (values_part, cols_part, count_part))  9.57 us
  transfers between devices with their start and end apart: 3, of which 2 were waited for; matrix products, arithmetic and copies ran while one was open for 33% of the time, Pallas kernels for 0%

profile of v1, /device:TPU:2, one launch (start us, length us, event | category | flops | bytes accessed | tf_op | source)
XLA Modules:
  0.0 304.1 jit_solution(18159632477161310236)
XLA Ops:
  6.5 3.5 %stack.2 = bf16[16,128,1024]{2,1,0:T(8,128)(2,1)} broadcast(bf16[128,1024]{1,0:T(8,128)(2,1)} %param.7), dimensions={1,2} | broadcast | bytes 4456448 | tf_op jit(solution)/shard_map/stack | solution.py:42
  10.0 11.6 %all-to-all-start = ((bf16[16,128,1024]{2,1,0:T(8,128)(2,1)}), bf16[16,128,1024]{2,1,0:T(8,128)(2,1)}, u32[]{:S(2)}, u32[]{:S(2)}) async-start(bf16[16,128,1024]{2,1,0:T(8,128)(2,1)} %stack.2), calls=%async_computation | async-start | bytes 8388608 | tf_op jit(solution)/shard_map/all_to_all | solution.py:41
  21.6 0.7 all-gather.2.cloned.1.call-update
  22.5 104.4 %all-to-all-done = bf16[16,128,1024]{2,1,0:T(8,128)(2,1)} async-done(((bf16[16,128,1024]{2,1,0:T(8,128)(2,1)}), bf16[16,128,1024]{2,1,0:T(8,128)(2,1)}, u32[]{:S(2)}, u32[]{:S(2)}) %all-to-all-start) | async-done | bytes 4194336 | tf_op jit(solution)/shard_map/all_to_all | solution.py:41
  126.9 100.4 %while.10 = (s32[]{:T(128)}, bf16[16,1,128,1024]{3,2,1,0:T(8,128)(2,1)}, s32[16,1]{0,1:T(1,128)S(1)}, bf16[16,1,8,128,128]{4,3,2,1,0:T(8,128)(2,1)}, s32[16,1,8]...) while((s32[]{:T(128)}, bf16[16,1,128,1024]{3,2,1,0:T(8,128)(2,1)}, s32[16,1]{0,1:T(1,128)S(1)}, ...), condition=%wide.region_1.2_spmd, body=%wide.region_0.1_spmd.sunk | while | flops 268567584 | bytes 7083249 | solution.py:29
  126.9 2.9 gather_fusion
  130.4 0.6 iota_compare_fusion.2
  131.0 2.2 fusion.17
  133.2 2.9 gather_fusion
  136.1 0.6 constant_dynamic-slice_fusion.3
  136.7 0.6 iota_compare_fusion.2
  137.3 2.2 fusion.17
  139.5 2.9 gather_fusion
  142.3 0.6 constant_dynamic-slice_fusion.3
  142.9 0.6 iota_compare_fusion.2
  143.6 2.2 fusion.17
  145.8 2.9 gather_fusion
  148.6 0.6 constant_dynamic-slice_fusion.3
  149.2 0.6 iota_compare_fusion.2
  149.9 2.2 fusion.17
  152.0 2.9 gather_fusion
  154.9 0.6 constant_dynamic-slice_fusion.3
  155.5 0.6 iota_compare_fusion.2
  156.1 2.1 fusion.17
  158.3 2.9 gather_fusion
  161.8 0.6 iota_compare_fusion.2
  162.4 2.2 fusion.17
  164.6 2.9 gather_fusion
  167.5 0.6 constant_dynamic-slice_fusion.3
  168.1 0.6 iota_compare_fusion.2
  168.7 2.2 fusion.17
  170.9 2.9 gather_fusion
  173.7 0.6 constant_dynamic-slice_fusion.3
  174.3 0.6 iota_compare_fusion.2
  175.0 2.2 fusion.17
  177.1 2.9 gather_fusion
  180.0 0.6 constant_dynamic-slice_fusion.3
  180.6 0.6 iota_compare_fusion.2
  181.2 2.2 fusion.17
  183.4 2.9 gather_fusion
  186.9 0.6 iota_compare_fusion.2
  187.5 2.2 fusion.17
  189.7 2.9 gather_fusion
  192.6 0.6 constant_dynamic-slice_fusion.3
  193.2 0.6 iota_compare_fusion.2
  193.8 2.2 fusion.17
  196.0 2.9 gather_fusion
  198.8 0.6 constant_dynamic-slice_fusion.3
  199.4 0.6 iota_compare_fusion.2
  200.1 2.2 fusion.17
  202.2 2.9 gather_fusion
  205.7 0.6 iota_compare_fusion.2
  206.3 2.2 fusion.17
  208.5 2.9 gather_fusion
  212.0 0.6 iota_compare_fusion.2
  212.6 2.2 fusion.17
  214.8 2.9 gather_fusion
  218.3 0.6 iota_compare_fusion.2
  218.9 2.1 fusion.17
  221.0 2.9 gather_fusion
  224.5 0.6 iota_compare_fusion.2
  225.2 2.2 fusion.17
  227.4 67.0 %reduce-scatter.2.cloned.1.call-done = bf16[128,1024]{1,0:T(8,128)(2,1)} async-done(((bf16[2048,1024]{1,0:T(8,128)(2,1)}), bf16[128,1024]{1,0:T(8,128)(2,1)}) %reduce-scatter.2.cloned.1.call-update) | async-done | bytes 262160 | tf_op jit(solution)/shard_map/reduce_scatter | solution.py:47
  294.4 2.8 fusion.8
  (49 shorter events, 4.6 us)
Async XLA Ops:
  10.0 12.4 %copy-start = (s32[1,1,16,8]{2,3,1,0:T(8,128)S(1)}, s32[1,1,16,8]{2,3,1,0:T(8,128)}, u32[]{:S(2)}) copy-start(s32[1,1,16,8]{2,3,1,0:T(8,128)} %param.10) | copy-start | bytes 1540
  10.0 116.9 %copy-start.1 = (s32[1,1,16]{2,1,0:T(1,128)S(1)}, s32[1,1,16]{2,1,0:T(1,128)}, u32[]{:S(2)}) copy-start(s32[1,1,16]{2,1,0:T(1,128)} %param.11) | copy-start | bytes 196
  10.0 116.9 %all-to-all-start = ((bf16[16,128,1024]{2,1,0:T(8,128)(2,1)}), bf16[16,128,1024]{2,1,0:T(8,128)(2,1)}, u32[]{:S(2)}, u32[]{:S(2)}) async-start(bf16[16,128,1024]{2,1,0:T(8,128)(2,1)} %stack.2), calls=%async_computation | async-start | bytes 8388608 | tf_op jit(solution)/shard_map/all_to_all | solution.py:41
  21.6 205.8 %all-gather.2.cloned.1.call-start = ((), (), s32[]{:S(2)}) async-start(), calls=%async_computation.3 | async-start | bytes 2228224 | tf_op jit(solution)/shard_map/all_gather | solution.py:55
  22.3 272.1 %reduce-scatter.2.cloned.1.call-start = ((), (), s32[]{:S(2)}) async-start(), calls=%async_computation.2 | async-start | bytes 4456448 | tf_op jit(solution)/shard_map/reduce_scatter | solution.py:47
Sparse Core Ops, SparseCore 0:
  24.3 64.3 all-gather.1
  227.5 66.9 reduce-scatter.1
